TPU v7x, 512 devices: a whole 4x8x8 slice. The times are simulated.
512 devices in a mesh: chan: 32 (over y_hi, z), win: 16 (over x, y_lo, core).
Axes of the slice: x: 4, y: 8 (y_hi: 4, y_lo: 2; y = y_hi * 2 + y_lo), z: 8, core: 2. Of those that a mesh axis runs over, the one named last changes fastest.
Arguments:
- traces: float32 [256, 196608], P('chan', 'win')
- offsets: int32 [16], P('win'), may hold values from 0 to 4096
- pair_source: int32 [32, 24], P('chan'), may hold values from 0 to 7
- pair_recv: int32 [32, 24], P('chan'), may hold values from 0 to 7
- pair_hop: int32 [32, 24], P('chan'), may hold values from 0 to 16, never falling along the last dimension, each value on 1 to 2 neighbouring positions
- pair_owner: int32 [768, 1], P('chan'), may hold values from 0 to 31; in each aligned block of 24 rows (0 to 23, 24 to 47, ...) at most 2 rows name the same one
Outputs:
- stacks: float32 [2048, 2, 2048], P('chan', None, 'win')
Inputs may be any that keep to these rules, and one draw needn't show every extreme that they name: `pair_hop`: within each block the pairs are ordered by offset index; every offset index has 1 to 2 pairs in a block, and some has exactly 2. `pair_owner`: at most 2 pairs of one block feed one owner, and some owner gets exactly 2.
All inputs are finite; a program needn't handle non-finite values.
Results may differ from a plain program's by a relative error of at most 0.022.
Values may be sent and summed in bfloat16 or wider, within the bound.
A program may use at most 128 MiB of HBM per device.

v0:
```python
import math

import jax
import jax.numpy as jnp
from jax import lax
from jax.sharding import PartitionSpec as P

NT = 8192
F = 2048
SMOOTH_HALF = 32
FX = 2112


def shifted(value, axis, by):
    peers = lax.axis_size(axis)
    return lax.ppermute(value, axis, [(i, (i + by) % peers) for i in range(peers)])


def transform(rows_data):
    count_rows = rows_data.shape[0]
    quarter = NT // 4
    outer_count = FX // 4
    corner = jnp.arange(4, dtype=jnp.int32)
    phase_four = (corner[:, None] * corner[None, :] % 4).astype(jnp.float32) * (math.pi / 2.0)
    cos_four = jnp.cos(phase_four)
    sin_four = jnp.sin(phase_four)
    folded = rows_data.reshape(count_rows, 4, quarter)
    first_real = jnp.einsum("rab,ak->rkb", folded, cos_four, precision=lax.Precision.HIGHEST)
    first_imag = -jnp.einsum("rab,ak->rkb", folded, sin_four, precision=lax.Precision.HIGHEST)
    inner = jnp.arange(quarter, dtype=jnp.int32)
    twist = (corner[:, None] * inner[None, :] % NT).astype(jnp.float32) * (2.0 * math.pi / NT)
    twist_cos = jnp.cos(twist)
    twist_sin = jnp.sin(twist)
    mixed_real = (first_real * twist_cos + first_imag * twist_sin).reshape(count_rows * 4, quarter)
    mixed_imag = (first_imag * twist_cos - first_real * twist_sin).reshape(count_rows * 4, quarter)
    outer = jnp.arange(outer_count, dtype=jnp.int32)
    table = (inner[:, None] * outer[None, :] % quarter).astype(jnp.float32) * (
        2.0 * math.pi / quarter
    )
    table_cos = jnp.cos(table)
    table_sin = jnp.sin(table)
    high = lax.Precision.HIGHEST
    out_real = jnp.dot(mixed_real, table_cos, precision=high) + jnp.dot(
        mixed_imag, table_sin, precision=high
    )
    out_imag = jnp.dot(mixed_imag, table_cos, precision=high) - jnp.dot(
        mixed_real, table_sin, precision=high
    )
    out_real = (
        out_real.reshape(count_rows, 4, outer_count).transpose(0, 2, 1).reshape(count_rows, FX)
    )
    out_imag = (
        out_imag.reshape(count_rows, 4, outer_count).transpose(0, 2, 1).reshape(count_rows, FX)
    )
    return (out_real, out_imag)


def whiten(segment):
    centred = segment - jnp.mean(segment, axis=1, keepdims=True)
    positions = jnp.arange(NT, dtype=jnp.int32).astype(jnp.float32)
    taper = 0.5 - 0.5 * jnp.cos(2.0 * math.pi / NT * positions)
    real_part, imag_part = transform(centred * taper)
    power = real_part * real_part + imag_part * imag_part
    level = lax.reduce_window(
        power, jnp.zeros((), power.dtype), lax.add, (1, 2 * SMOOTH_HALF + 1), (1, 1), "VALID"
    ) / (2 * SMOOTH_HALF + 1)
    scale = lax.rsqrt(level + 1e-06)
    kept_real = real_part[:, SMOOTH_HALF : SMOOTH_HALF + F] * scale
    kept_imag = imag_part[:, SMOOTH_HALF : SMOOTH_HALF + F] * scale
    return jnp.stack([kept_real, kept_imag], axis=1).astype(jnp.bfloat16)


def forward_move(carried):
    return shifted(carried, "chan", 1)


def local(traces, offsets, pair_source, pair_recv, pair_hop, pair_owner):
    chan_count = lax.axis_size("chan")
    local_channels = traces.shape[0]
    local_windows = offsets.shape[0]
    pair_slots = pair_source.shape[1]
    reach_blocks = min(8, (chan_count - 1) // 2)
    offset_count = 2 * reach_blocks + 1
    run_rows = 2 * pair_slots // offset_count
    capacity = 2 * ((pair_slots + chan_count - 1) // chan_count)
    segment = jnp.stack([lax.dynamic_slice_in_dim(traces, offsets[0], NT, 1)], axis=1)
    white = whiten(segment.reshape(local_channels * local_windows, NT))
    white = white.reshape(local_channels, local_windows, 2, F)
    source_list = pair_source.reshape(-1)
    receiver_list = pair_recv.reshape(-1)
    hop_list = pair_hop.reshape(-1)
    owner_list = pair_owner.reshape(-1)
    offset_ids = jnp.arange(offset_count, dtype=jnp.int32)
    starts = jnp.sum((hop_list[None, :] < offset_ids[:, None]).astype(jnp.int32), axis=1)

    def offset_terms(carried, offset_index):
        before = jnp.take(starts, offset_index)
        positions = before + jnp.arange(run_rows, dtype=jnp.int32)
        clipped = jnp.minimum(positions, pair_slots - 1)
        source_rows = jnp.take(white, jnp.take(source_list, clipped), axis=0).astype(jnp.float32)
        receiver_rows = jnp.take(carried, jnp.take(receiver_list, clipped), axis=0).astype(
            jnp.float32
        )
        real_part = jnp.sum(
            source_rows[:, :, 0] * receiver_rows[:, :, 0]
            + source_rows[:, :, 1] * receiver_rows[:, :, 1],
            axis=1,
        )
        imag_part = jnp.sum(
            source_rows[:, :, 0] * receiver_rows[:, :, 1]
            - source_rows[:, :, 1] * receiver_rows[:, :, 0],
            axis=1,
        )
        return jnp.stack([real_part, imag_part], axis=1)

    local_terms = offset_terms(white, jnp.int32(reach_blocks))

    def advance(carried, index):
        carried = forward_move(carried)
        offset_index = jnp.where(
            index <= reach_blocks, reach_blocks - index, reach_blocks + chan_count - index
        )
        offset_index = jnp.clip(offset_index, 0, offset_count - 1)
        return (carried, offset_terms(carried, offset_index))

    unused, moved_terms = lax.scan(advance, white, jnp.arange(1, chan_count, dtype=jnp.int32))
    collected = jnp.concatenate([local_terms[None], moved_terms], axis=0)
    position = jnp.where(
        hop_list == reach_blocks,
        0,
        jnp.where(
            hop_list < reach_blocks, reach_blocks - hop_list, reach_blocks + chan_count - hop_list
        ),
    )
    rank = jnp.arange(pair_slots, dtype=jnp.int32) - jnp.take(starts, hop_list)
    flat_rows = position * run_rows + rank
    band = collected.shape[-1]
    totals = jnp.take(collected.reshape(-1, 2, band), flat_rows, axis=0)
    partial_value = lax.optimization_barrier(totals.astype(jnp.bfloat16))
    onehot = (owner_list[:, None] == jnp.arange(chan_count, dtype=jnp.int32)[None, :]).astype(
        jnp.int32
    )
    earlier = jnp.cumsum(onehot, axis=0) - onehot
    slot = jnp.sum(earlier * onehot, axis=1)
    target = owner_list * capacity + slot
    dispatch = jnp.arange(chan_count * capacity, dtype=jnp.int32)[:, None] == target[None, :]
    outgoing = jnp.dot(
        dispatch.astype(jnp.bfloat16),
        partial_value.reshape(pair_slots, 2 * F),
        preferred_element_type=jnp.float32,
    )
    outgoing = outgoing.astype(jnp.bfloat16).reshape(chan_count, capacity, 2, F)
    arrived = lax.all_to_all(outgoing, "chan", split_axis=0, concat_axis=0, tiled=True)
    summed = lax.psum_scatter(
        arrived.astype(jnp.float32).astype(jnp.bfloat16), "win", scatter_dimension=3, tiled=True
    ).astype(jnp.float32)
    return summed.reshape(chan_count * capacity, 2, summed.shape[3])


def solution(mesh):
    placed = (
        P("chan", "win"),
        P("win"),
        P("chan", None),
        P("chan", None),
        P("chan", None),
        P("chan", None),
    )
    return jax.shard_map(
        local, mesh=mesh, in_specs=placed, out_specs=P("chan", None, "win"), check_vma=False
    )
```

profile of v0, /device:TPU:1, one launch (start us, length us, event | category | flops | bytes accessed | tf_op | source)
XLA Modules:
  0.0 716.3 jit_solution(1198854006266639592)
XLA Ops:
  15.6 22.8 %fusion.13 = f32[32,528]{1,0:T(8,128)S(1)} fusion(f32[32,2048]{1,0:T(8,128)S(1)} %reshape.523), kind=kOutput, calls=%fused_computation.40 | convolution fusion | flops 430374912 | bytes 329728 | tf_op jit(solution)/shard_map/dot_general | solution.py:43
  38.5 22.5 %fusion.11 = f32[32,528]{1,0:T(8,128)S(1)} fusion(f32[32,2048]{1,0:T(8,128)S(1)} %reshape.524), kind=kOutput, calls=%fused_computation.39 | convolution fusion | flops 430374912 | bytes 329728 | tf_op jit(solution)/shard_map/dot_general | solution.py:46
  61.0 23.2 %fusion.19 = f32[32,528]{1,0:T(8,128)S(1)} fusion(f32[32,528]{1,0:T(8,128)S(1)} %fusion.13, f32[32,2048]{1,0:T(8,128)S(1)} %reshape.524), kind=kOutput, calls=%fused_computation.44 | convolution fusion | flops 430391808 | bytes 397312 | tf_op jit(solution)/shard_map/dot_general | solution.py:43
  84.1 22.8 %fusion.22 = f32[32,528]{1,0:T(8,128)S(1)} fusion(f32[32,528]{1,0:T(8,128)S(1)} %fusion.11, f32[32,2048]{1,0:T(8,128)S(1)} %reshape.523), kind=kOutput, calls=%fused_computation.45 | convolution fusion | flops 430391808 | bytes 397312 | tf_op jit(solution)/shard_map/dot_general | solution.py:46
  113.8 18.3 %reduce_window.7 = f32[8,2048]{1,0:T(8,128)S(1)} reduce-window(f32[8,2112]{1,0:T(8,128)S(1)} %copy.49, f32[]{:T(128)} %constant.167.clone.1), window={size=1x65}, to_apply=%region_4.5 | reduce-window | flops 1048576 | bytes 133124 | tf_op jit(solution)/shard_map/reduce_window | solution.py:64
  134.2 342.2 %while.14 = (s32[]{:T(128)}, bf16[8,1,2,2048]{3,2,1,0:T(2,128)(2,1)S(1)}, bf16[31,2,2,2048]{3,2,1,0:T(2,128)(2,1)}, s32[31]{0:T(128)S(1)}, s32[17]{0:T(128)S(1)}...) while((s32[]{:T(128)}, ...), condition=%wide.region_6.9_spmd, body=%wide.region_5.8_spmd.sunk | while | flops 101456 | bytes 684481 | solution.py:126
  134.2 4.8 collective-permute-start
  144.9 6.2 collective-permute-done
  152.6 1.9 collective-permute-start
  163.5 1.9 collective-permute-start
  174.2 1.9 collective-permute-start
  184.9 1.9 collective-permute-start
  195.6 1.9 collective-permute-start
  206.3 1.9 collective-permute-start
  217.0 1.9 collective-permute-start
  227.7 1.9 collective-permute-start
  238.7 1.9 collective-permute-start
  249.7 1.9 collective-permute-start
  260.5 1.9 collective-permute-start
  271.2 1.9 collective-permute-start
  281.9 1.9 collective-permute-start
  292.6 1.9 collective-permute-start
  303.3 1.9 collective-permute-start
  324.7 1.9 collective-permute-start
  439.7 2.2 collective-permute-done
  462.1 2.1 collective-permute-done
  480.0 19.3 %all_to_all.5 = bf16[32,2,2,2048]{3,2,1,0:T(2,128)(2,1)S(1)} all-to-all(bf16[32,2,2,2048]{3,2,1,0:T(2,128)(2,1)S(1)} %reshape.533), channel_id=1, replica_groups=mesh['chan'=32,'win'=16] {'chan'}, dimensions={0} | all-to-all | bytes 1048576 | tf_op jit(solution)/shard_map/all_to_all | solution.py:153
  499.4 55.7 %copy.59 = bf16[32,2,2,2048]{2,1,0,3:T(2,128)(2,1)} copy(bf16[32,2,2,2048]{3,2,1,0:T(2,128)(2,1)S(1)} %all_to_all.5) | data formatting | bytes 1048576
  555.0 49.3 %reshape.703 = bf16[2048,128]{1,0:T(8,128)(2,1)} reshape(bf16[2048,32,2,2]{3,2,1,0:T(2,128)(2,1)} %bitcast.129) | data formatting | bytes 1048576
  604.3 97.0 %reduce-scatter.4.cloned.1.call-done = bf16[128,128]{1,0:T(8,128)(2,1)} async-done(((bf16[2048,128]{1,0:T(8,128)(2,1)}), bf16[128,128]{1,0:T(8,128)(2,1)}) %reduce-scatter.4.cloned.1.call-update) | async-done | bytes 32784
  701.3 5.2 reshape.704
  706.6 2.0 copy.60
  (605 shorter events, 233.2 us)
Async XLA Ops:
  6.5 694.8 %reduce-scatter.4.cloned.1.call-start = ((), (), s32[]{:S(2)}) async-start(), calls=%async_computation.2 | async-start | bytes 557056
  134.2 16.9 %collective-permute-start = (bf16[8,1,2,2048]{3,2,1,0:T(2,128)(2,1)S(1)}, bf16[8,1,2,2048]{3,2,1,0:T(2,128)(2,1)S(1)}, u32[]{:S(2)}, u32[]{:S(2)}) collective-permute-start(bf16[8,1,2,2048]{3,2,1,0:T(2,128)(2,1)S(1)} %get-tuple-element.222), channel_id=1, source_target_pairs={{0,16},{16,32},{32,48},{48,64},{64,80},{80,96},{96,112},{112,128},... | collective-permute-start | bytes 196616 | tf_op jit(solution)/shard_map/while/body/eval_jaxpr/ppermute | solution.py:16
  152.6 9.5 %collective-permute-start = (bf16[8,1,2,2048]{3,2,1,0:T(2,128)(2,1)S(1)}, bf16[8,1,2,2048]{3,2,1,0:T(2,128)(2,1)S(1)}, u32[]{:S(2)}, u32[]{:S(2)}) collective-permute-start(bf16[8,1,2,2048]{3,2,1,0:T(2,128)(2,1)S(1)} %get-tuple-element.222), channel_id=1, source_target_pairs={{0,16},{16,32},{32,48},{48,64},{64,80},{80,96},{96,112},{112,128},... | collective-permute-start | bytes 196616 | tf_op jit(solution)/shard_map/while/body/eval_jaxpr/ppermute | solution.py:16
  163.5 9.2 %collective-permute-start = (bf16[8,1,2,2048]{3,2,1,0:T(2,128)(2,1)S(1)}, bf16[8,1,2,2048]{3,2,1,0:T(2,128)(2,1)S(1)}, u32[]{:S(2)}, u32[]{:S(2)}) collective-permute-start(bf16[8,1,2,2048]{3,2,1,0:T(2,128)(2,1)S(1)} %get-tuple-element.222), channel_id=1, source_target_pairs={{0,16},{16,32},{32,48},{48,64},{64,80},{80,96},{96,112},{112,128},... | collective-permute-start | bytes 196616 | tf_op jit(solution)/shard_map/while/body/eval_jaxpr/ppermute | solution.py:16
  174.2 9.2 %collective-permute-start = (bf16[8,1,2,2048]{3,2,1,0:T(2,128)(2,1)S(1)}, bf16[8,1,2,2048]{3,2,1,0:T(2,128)(2,1)S(1)}, u32[]{:S(2)}, u32[]{:S(2)}) collective-permute-start(bf16[8,1,2,2048]{3,2,1,0:T(2,128)(2,1)S(1)} %get-tuple-element.222), channel_id=1, source_target_pairs={{0,16},{16,32},{32,48},{48,64},{64,80},{80,96},{96,112},{112,128},... | collective-permute-start | bytes 196616 | tf_op jit(solution)/shard_map/while/body/eval_jaxpr/ppermute | solution.py:16
  184.9 9.2 %collective-permute-start = (bf16[8,1,2,2048]{3,2,1,0:T(2,128)(2,1)S(1)}, bf16[8,1,2,2048]{3,2,1,0:T(2,128)(2,1)S(1)}, u32[]{:S(2)}, u32[]{:S(2)}) collective-permute-start(bf16[8,1,2,2048]{3,2,1,0:T(2,128)(2,1)S(1)} %get-tuple-element.222), channel_id=1, source_target_pairs={{0,16},{16,32},{32,48},{48,64},{64,80},{80,96},{96,112},{112,128},... | collective-permute-start | bytes 196616 | tf_op jit(solution)/shard_map/while/body/eval_jaxpr/ppermute | solution.py:16
  195.6 9.2 %collective-permute-start = (bf16[8,1,2,2048]{3,2,1,0:T(2,128)(2,1)S(1)}, bf16[8,1,2,2048]{3,2,1,0:T(2,128)(2,1)S(1)}, u32[]{:S(2)}, u32[]{:S(2)}) collective-permute-start(bf16[8,1,2,2048]{3,2,1,0:T(2,128)(2,1)S(1)} %get-tuple-element.222), channel_id=1, source_target_pairs={{0,16},{16,32},{32,48},{48,64},{64,80},{80,96},{96,112},{112,128},... | collective-permute-start | bytes 196616 | tf_op jit(solution)/shard_map/while/body/eval_jaxpr/ppermute | solution.py:16
  206.3 9.2 %collective-permute-start = (bf16[8,1,2,2048]{3,2,1,0:T(2,128)(2,1)S(1)}, bf16[8,1,2,2048]{3,2,1,0:T(2,128)(2,1)S(1)}, u32[]{:S(2)}, u32[]{:S(2)}) collective-permute-start(bf16[8,1,2,2048]{3,2,1,0:T(2,128)(2,1)S(1)} %get-tuple-element.222), channel_id=1, source_target_pairs={{0,16},{16,32},{32,48},{48,64},{64,80},{80,96},{96,112},{112,128},... | collective-permute-start | bytes 196616 | tf_op jit(solution)/shard_map/while/body/eval_jaxpr/ppermute | solution.py:16
  217.0 9.2 %collective-permute-start = (bf16[8,1,2,2048]{3,2,1,0:T(2,128)(2,1)S(1)}, bf16[8,1,2,2048]{3,2,1,0:T(2,128)(2,1)S(1)}, u32[]{:S(2)}, u32[]{:S(2)}) collective-permute-start(bf16[8,1,2,2048]{3,2,1,0:T(2,128)(2,1)S(1)} %get-tuple-element.222), channel_id=1, source_target_pairs={{0,16},{16,32},{32,48},{48,64},{64,80},{80,96},{96,112},{112,128},... | collective-permute-start | bytes 196616 | tf_op jit(solution)/shard_map/while/body/eval_jaxpr/ppermute | solution.py:16
  227.7 9.5 %collective-permute-start = (bf16[8,1,2,2048]{3,2,1,0:T(2,128)(2,1)S(1)}, bf16[8,1,2,2048]{3,2,1,0:T(2,128)(2,1)S(1)}, u32[]{:S(2)}, u32[]{:S(2)}) collective-permute-start(bf16[8,1,2,2048]{3,2,1,0:T(2,128)(2,1)S(1)} %get-tuple-element.222), channel_id=1, source_target_pairs={{0,16},{16,32},{32,48},{48,64},{64,80},{80,96},{96,112},{112,128},... | collective-permute-start | bytes 196616 | tf_op jit(solution)/shard_map/while/body/eval_jaxpr/ppermute | solution.py:16
  238.7 9.6 %collective-permute-start = (bf16[8,1,2,2048]{3,2,1,0:T(2,128)(2,1)S(1)}, bf16[8,1,2,2048]{3,2,1,0:T(2,128)(2,1)S(1)}, u32[]{:S(2)}, u32[]{:S(2)}) collective-permute-start(bf16[8,1,2,2048]{3,2,1,0:T(2,128)(2,1)S(1)} %get-tuple-element.222), channel_id=1, source_target_pairs={{0,16},{16,32},{32,48},{48,64},{64,80},{80,96},{96,112},{112,128},... | collective-permute-start | bytes 196616 | tf_op jit(solution)/shard_map/while/body/eval_jaxpr/ppermute | solution.py:16
  249.7 9.3 %collective-permute-start = (bf16[8,1,2,2048]{3,2,1,0:T(2,128)(2,1)S(1)}, bf16[8,1,2,2048]{3,2,1,0:T(2,128)(2,1)S(1)}, u32[]{:S(2)}, u32[]{:S(2)}) collective-permute-start(bf16[8,1,2,2048]{3,2,1,0:T(2,128)(2,1)S(1)} %get-tuple-element.222), channel_id=1, source_target_pairs={{0,16},{16,32},{32,48},{48,64},{64,80},{80,96},{96,112},{112,128},... | collective-permute-start | bytes 196616 | tf_op jit(solution)/shard_map/while/body/eval_jaxpr/ppermute | solution.py:16
  260.5 9.2 %collective-permute-start = (bf16[8,1,2,2048]{3,2,1,0:T(2,128)(2,1)S(1)}, bf16[8,1,2,2048]{3,2,1,0:T(2,128)(2,1)S(1)}, u32[]{:S(2)}, u32[]{:S(2)}) collective-permute-start(bf16[8,1,2,2048]{3,2,1,0:T(2,128)(2,1)S(1)} %get-tuple-element.222), channel_id=1, source_target_pairs={{0,16},{16,32},{32,48},{48,64},{64,80},{80,96},{96,112},{112,128},... | collective-permute-start | bytes 196616 | tf_op jit(solution)/shard_map/while/body/eval_jaxpr/ppermute | solution.py:16
  271.2 9.2 %collective-permute-start = (bf16[8,1,2,2048]{3,2,1,0:T(2,128)(2,1)S(1)}, bf16[8,1,2,2048]{3,2,1,0:T(2,128)(2,1)S(1)}, u32[]{:S(2)}, u32[]{:S(2)}) collective-permute-start(bf16[8,1,2,2048]{3,2,1,0:T(2,128)(2,1)S(1)} %get-tuple-element.222), channel_id=1, source_target_pairs={{0,16},{16,32},{32,48},{48,64},{64,80},{80,96},{96,112},{112,128},... | collective-permute-start | bytes 196616 | tf_op jit(solution)/shard_map/while/body/eval_jaxpr/ppermute | solution.py:16
  281.9 9.2 %collective-permute-start = (bf16[8,1,2,2048]{3,2,1,0:T(2,128)(2,1)S(1)}, bf16[8,1,2,2048]{3,2,1,0:T(2,128)(2,1)S(1)}, u32[]{:S(2)}, u32[]{:S(2)}) collective-permute-start(bf16[8,1,2,2048]{3,2,1,0:T(2,128)(2,1)S(1)} %get-tuple-element.222), channel_id=1, source_target_pairs={{0,16},{16,32},{32,48},{48,64},{64,80},{80,96},{96,112},{112,128},... | collective-permute-start | bytes 196616 | tf_op jit(solution)/shard_map/while/body/eval_jaxpr/ppermute | solution.py:16
  292.6 9.2 %collective-permute-start = (bf16[8,1,2,2048]{3,2,1,0:T(2,128)(2,1)S(1)}, bf16[8,1,2,2048]{3,2,1,0:T(2,128)(2,1)S(1)}, u32[]{:S(2)}, u32[]{:S(2)}) collective-permute-start(bf16[8,1,2,2048]{3,2,1,0:T(2,128)(2,1)S(1)} %get-tuple-element.222), channel_id=1, source_target_pairs={{0,16},{16,32},{32,48},{48,64},{64,80},{80,96},{96,112},{112,128},... | collective-permute-start | bytes 196616 | tf_op jit(solution)/shard_map/while/body/eval_jaxpr/ppermute | solution.py:16
  303.3 9.2 %collective-permute-start = (bf16[8,1,2,2048]{3,2,1,0:T(2,128)(2,1)S(1)}, bf16[8,1,2,2048]{3,2,1,0:T(2,128)(2,1)S(1)}, u32[]{:S(2)}, u32[]{:S(2)}) collective-permute-start(bf16[8,1,2,2048]{3,2,1,0:T(2,128)(2,1)S(1)} %get-tuple-element.222), channel_id=1, source_target_pairs={{0,16},{16,32},{32,48},{48,64},{64,80},{80,96},{96,112},{112,128},... | collective-permute-start | bytes 196616 | tf_op jit(solution)/shard_map/while/body/eval_jaxpr/ppermute | solution.py:16
  314.0 9.2 %collective-permute-start = (bf16[8,1,2,2048]{3,2,1,0:T(2,128)(2,1)S(1)}, bf16[8,1,2,2048]{3,2,1,0:T(2,128)(2,1)S(1)}, u32[]{:S(2)}, u32[]{:S(2)}) collective-permute-start(bf16[8,1,2,2048]{3,2,1,0:T(2,128)(2,1)S(1)} %get-tuple-element.222), channel_id=1, source_target_pairs={{0,16},{16,32},{32,48},{48,64},{64,80},{80,96},{96,112},{112,128},... | collective-permute-start | bytes 196616 | tf_op jit(solution)/shard_map/while/body/eval_jaxpr/ppermute | solution.py:16
  324.7 9.4 %collective-permute-start = (bf16[8,1,2,2048]{3,2,1,0:T(2,128)(2,1)S(1)}, bf16[8,1,2,2048]{3,2,1,0:T(2,128)(2,1)S(1)}, u32[]{:S(2)}, u32[]{:S(2)}) collective-permute-start(bf16[8,1,2,2048]{3,2,1,0:T(2,128)(2,1)S(1)} %get-tuple-element.222), channel_id=1, source_target_pairs={{0,16},{16,32},{32,48},{48,64},{64,80},{80,96},{96,112},{112,128},... | collective-permute-start | bytes 196616 | tf_op jit(solution)/shard_map/while/body/eval_jaxpr/ppermute | solution.py:16
  335.6 9.2 %collective-permute-start = (bf16[8,1,2,2048]{3,2,1,0:T(2,128)(2,1)S(1)}, bf16[8,1,2,2048]{3,2,1,0:T(2,128)(2,1)S(1)}, u32[]{:S(2)}, u32[]{:S(2)}) collective-permute-start(bf16[8,1,2,2048]{3,2,1,0:T(2,128)(2,1)S(1)} %get-tuple-element.222), channel_id=1, source_target_pairs={{0,16},{16,32},{32,48},{48,64},{64,80},{80,96},{96,112},{112,128},... | collective-permute-start | bytes 196616 | tf_op jit(solution)/shard_map/while/body/eval_jaxpr/ppermute | solution.py:16
  346.3 9.2 %collective-permute-start = (bf16[8,1,2,2048]{3,2,1,0:T(2,128)(2,1)S(1)}, bf16[8,1,2,2048]{3,2,1,0:T(2,128)(2,1)S(1)}, u32[]{:S(2)}, u32[]{:S(2)}) collective-permute-start(bf16[8,1,2,2048]{3,2,1,0:T(2,128)(2,1)S(1)} %get-tuple-element.222), channel_id=1, source_target_pairs={{0,16},{16,32},{32,48},{48,64},{64,80},{80,96},{96,112},{112,128},... | collective-permute-start | bytes 196616 | tf_op jit(solution)/shard_map/while/body/eval_jaxpr/ppermute | solution.py:16
  357.0 9.3 %collective-permute-start = (bf16[8,1,2,2048]{3,2,1,0:T(2,128)(2,1)S(1)}, bf16[8,1,2,2048]{3,2,1,0:T(2,128)(2,1)S(1)}, u32[]{:S(2)}, u32[]{:S(2)}) collective-permute-start(bf16[8,1,2,2048]{3,2,1,0:T(2,128)(2,1)S(1)} %get-tuple-element.222), channel_id=1, source_target_pairs={{0,16},{16,32},{32,48},{48,64},{64,80},{80,96},{96,112},{112,128},... | collective-permute-start | bytes 196616 | tf_op jit(solution)/shard_map/while/body/eval_jaxpr/ppermute | solution.py:16
  367.7 9.2 %collective-permute-start = (bf16[8,1,2,2048]{3,2,1,0:T(2,128)(2,1)S(1)}, bf16[8,1,2,2048]{3,2,1,0:T(2,128)(2,1)S(1)}, u32[]{:S(2)}, u32[]{:S(2)}) collective-permute-start(bf16[8,1,2,2048]{3,2,1,0:T(2,128)(2,1)S(1)} %get-tuple-element.222), channel_id=1, source_target_pairs={{0,16},{16,32},{32,48},{48,64},{64,80},{80,96},{96,112},{112,128},... | collective-permute-start | bytes 196616 | tf_op jit(solution)/shard_map/while/body/eval_jaxpr/ppermute | solution.py:16
  378.4 9.2 %collective-permute-start = (bf16[8,1,2,2048]{3,2,1,0:T(2,128)(2,1)S(1)}, bf16[8,1,2,2048]{3,2,1,0:T(2,128)(2,1)S(1)}, u32[]{:S(2)}, u32[]{:S(2)}) collective-permute-start(bf16[8,1,2,2048]{3,2,1,0:T(2,128)(2,1)S(1)} %get-tuple-element.222), channel_id=1, source_target_pairs={{0,16},{16,32},{32,48},{48,64},{64,80},{80,96},{96,112},{112,128},... | collective-permute-start | bytes 196616 | tf_op jit(solution)/shard_map/while/body/eval_jaxpr/ppermute | solution.py:16
  389.1 9.2 %collective-permute-start = (bf16[8,1,2,2048]{3,2,1,0:T(2,128)(2,1)S(1)}, bf16[8,1,2,2048]{3,2,1,0:T(2,128)(2,1)S(1)}, u32[]{:S(2)}, u32[]{:S(2)}) collective-permute-start(bf16[8,1,2,2048]{3,2,1,0:T(2,128)(2,1)S(1)} %get-tuple-element.222), channel_id=1, source_target_pairs={{0,16},{16,32},{32,48},{48,64},{64,80},{80,96},{96,112},{112,128},... | collective-permute-start | bytes 196616 | tf_op jit(solution)/shard_map/while/body/eval_jaxpr/ppermute | solution.py:16
  399.8 9.2 %collective-permute-start = (bf16[8,1,2,2048]{3,2,1,0:T(2,128)(2,1)S(1)}, bf16[8,1,2,2048]{3,2,1,0:T(2,128)(2,1)S(1)}, u32[]{:S(2)}, u32[]{:S(2)}) collective-permute-start(bf16[8,1,2,2048]{3,2,1,0:T(2,128)(2,1)S(1)} %get-tuple-element.222), channel_id=1, source_target_pairs={{0,16},{16,32},{32,48},{48,64},{64,80},{80,96},{96,112},{112,128},... | collective-permute-start | bytes 196616 | tf_op jit(solution)/shard_map/while/body/eval_jaxpr/ppermute | solution.py:16
  410.5 9.2 %collective-permute-start = (bf16[8,1,2,2048]{3,2,1,0:T(2,128)(2,1)S(1)}, bf16[8,1,2,2048]{3,2,1,0:T(2,128)(2,1)S(1)}, u32[]{:S(2)}, u32[]{:S(2)}) collective-permute-start(bf16[8,1,2,2048]{3,2,1,0:T(2,128)(2,1)S(1)} %get-tuple-element.222), channel_id=1, source_target_pairs={{0,16},{16,32},{32,48},{48,64},{64,80},{80,96},{96,112},{112,128},... | collective-permute-start | bytes 196616 | tf_op jit(solution)/shard_map/while/body/eval_jaxpr/ppermute | solution.py:16
  421.2 9.3 %collective-permute-start = (bf16[8,1,2,2048]{3,2,1,0:T(2,128)(2,1)S(1)}, bf16[8,1,2,2048]{3,2,1,0:T(2,128)(2,1)S(1)}, u32[]{:S(2)}, u32[]{:S(2)}) collective-permute-start(bf16[8,1,2,2048]{3,2,1,0:T(2,128)(2,1)S(1)} %get-tuple-element.222), channel_id=1, source_target_pairs={{0,16},{16,32},{32,48},{48,64},{64,80},{80,96},{96,112},{112,128},... | collective-permute-start | bytes 196616 | tf_op jit(solution)/shard_map/while/body/eval_jaxpr/ppermute | solution.py:16
  431.9 10.0 %collective-permute-start = (bf16[8,1,2,2048]{3,2,1,0:T(2,128)(2,1)S(1)}, bf16[8,1,2,2048]{3,2,1,0:T(2,128)(2,1)S(1)}, u32[]{:S(2)}, u32[]{:S(2)}) collective-permute-start(bf16[8,1,2,2048]{3,2,1,0:T(2,128)(2,1)S(1)} %get-tuple-element.222), channel_id=1, source_target_pairs={{0,16},{16,32},{32,48},{48,64},{64,80},{80,96},{96,112},{112,128},... | collective-permute-start | bytes 196616 | tf_op jit(solution)/shard_map/while/body/eval_jaxpr/ppermute | solution.py:16
  443.4 9.4 %collective-permute-start = (bf16[8,1,2,2048]{3,2,1,0:T(2,128)(2,1)S(1)}, bf16[8,1,2,2048]{3,2,1,0:T(2,128)(2,1)S(1)}, u32[]{:S(2)}, u32[]{:S(2)}) collective-permute-start(bf16[8,1,2,2048]{3,2,1,0:T(2,128)(2,1)S(1)} %get-tuple-element.222), channel_id=1, source_target_pairs={{0,16},{16,32},{32,48},{48,64},{64,80},{80,96},{96,112},{112,128},... | collective-permute-start | bytes 196616 | tf_op jit(solution)/shard_map/while/body/eval_jaxpr/ppermute | solution.py:16
  454.3 9.9 %collective-permute-start = (bf16[8,1,2,2048]{3,2,1,0:T(2,128)(2,1)S(1)}, bf16[8,1,2,2048]{3,2,1,0:T(2,128)(2,1)S(1)}, u32[]{:S(2)}, u32[]{:S(2)}) collective-permute-start(bf16[8,1,2,2048]{3,2,1,0:T(2,128)(2,1)S(1)} %get-tuple-element.222), channel_id=1, source_target_pairs={{0,16},{16,32},{32,48},{48,64},{64,80},{80,96},{96,112},{112,128},... | collective-permute-start | bytes 196616 | tf_op jit(solution)/shard_map/while/body/eval_jaxpr/ppermute | solution.py:16
  465.7 9.2 %collective-permute-start = (bf16[8,1,2,2048]{3,2,1,0:T(2,128)(2,1)S(1)}, bf16[8,1,2,2048]{3,2,1,0:T(2,128)(2,1)S(1)}, u32[]{:S(2)}, u32[]{:S(2)}) collective-permute-start(bf16[8,1,2,2048]{3,2,1,0:T(2,128)(2,1)S(1)} %get-tuple-element.222), channel_id=1, source_target_pairs={{0,16},{16,32},{32,48},{48,64},{64,80},{80,96},{96,112},{112,128},... | collective-permute-start | bytes 196616 | tf_op jit(solution)/shard_map/while/body/eval_jaxpr/ppermute | solution.py:16
  (3 other events, 31.0 us)
Sparse Core Ops, SparseCore 0:
  604.4 96.8 reduce-scatter.3
where the time goes:
time: 723 us; the launch traced here: 716 us
  local copies, waits for them, and re-layouts  238 us (33%)
  waiting for transfers between devices  150 us (21%)
  matrix products  93 us (13%)
  loops' own time  84.4 us (12%)
  starting transfers between devices  62.4 us (9%)
  other arithmetic  54.6 us (8%)
  blocking collectives  19.3 us (3%)
  between operations  14.6 us (2%)
    unnamed x15, local copies, waits for them, and re-layouts  115 us
    unnamed x2, waiting for transfers between devices  97 us
    another operation x1, loops' own time, local(): lax.scan(advance, white, jnp.arange(1, chan_count, dtype=jnp.int32))  84.4 us
    ppermute x31, starting transfers between devices, shifted(): lax.ppermute(value, axis, [(i, (i + by) % peers) for i in range(peers)])  62.4 us
    ppermute x31, waiting for transfers between devices, shifted(): lax.ppermute(value, axis, [(i, (i + by) % peers) for i in range(peers)])  52.7 us
    dot_general x1, matrix products, transform(): jnp.dot(mixed_imag, table_sin, precision=high)  23.2 us
    dot_general x1, matrix products, transform(): jnp.dot(mixed_real, table_sin, precision=high)  22.8 us
    dot_general x1, matrix products, transform(): jnp.dot(mixed_real, table_cos, precision=high)  22.8 us
  transfers between devices with their start and end apart: 32, of which 32 were waited for; matrix products, arithmetic and copies ran while one was open for 14% of the time, Pallas kernels for 0%

commit v1 on v0

v1 whole, which is shorter than its diff:
```python
import jax
import jax.numpy as jnp
import numpy as np
from jax import lax
from jax.experimental import pallas as pl
from jax.experimental.pallas import tpu as pltpu
from jax.sharding import PartitionSpec as P

MESH = pl.DeviceIdType.MESH
NT = 8192
LANES = 128
ROWS = NT // LANES
BANDS = 16
HALF = 32
CH = 8
NWIN = 16
NCHAN = 32
HOPS = 8
OFFS = 17
PAIRS = 24
REC = 12288
F32 = jnp.float32
BF16 = jnp.bfloat16
HIGH = lax.Precision.HIGHEST


def tables():
    lane = np.arange(LANES)
    row = np.arange(ROWS)
    low = lane + HALF
    angle = 2.0 * np.pi / ROWS * (np.outer(low, row) % ROWS)
    first = np.concatenate([np.cos(angle), -np.sin(angle)], axis=0)
    angle = 2.0 * np.pi / NT * (np.outer(low, lane) % NT)
    twist = np.stack([np.cos(angle), -np.sin(angle)])
    band = np.arange(-1, BANDS + 1)
    angle = 2.0 * np.pi / ROWS * (np.outer(band, lane) % ROWS)
    cos, sin = np.cos(angle), np.sin(angle)
    pad = np.zeros((6, 2 * LANES))
    second = np.concatenate(
        [np.concatenate([cos, sin], axis=1), pad, np.concatenate([-sin, cos], axis=1), pad], axis=0
    )
    place = np.arange(NT).reshape(ROWS, LANES)
    hann = 0.5 - 0.5 * np.cos(2.0 * np.pi / NT * place)
    order = np.zeros((256, 256))
    for ch in range(CH):
        for part in range(2):
            for w in range(NWIN):
                order[ch * 32 + part * 16 + w, w * 16 + part * 8 + ch] = 1.0
    return (
        first.astype(np.float32),
        twist.astype(np.float32),
        second.astype(np.float32),
        hann.astype(np.float32),
        order.astype(jnp.bfloat16),
    )


def kernel(
    offset_ref, source_ref, receiver_ref, hop_ref, owner_ref,
    x_ref, first_ref, twist_ref, second_ref, hann_ref, order_ref,
    out_ref,
    seg_ref, spec_ref, white_ref, all_ref, rows_ref, send_ref, got_ref, cross_ref, mail_ref,
    ask_ref, asked_ref,
    ask_send, ask_recv, win_send, win_recv, hop_send, hop_recv, own_send, own_recv,
):
    mc = lax.axis_index("chan")
    mw = lax.axis_index("win")

    barrier = pltpu.get_barrier_semaphore()

    def greet_win(j, carry):
        pl.semaphore_signal(barrier, inc=1, device_id=(mc, lax.rem(mw + j, NWIN)), device_id_type=MESH)
        return carry

    def greet_chan(j, carry):
        pl.semaphore_signal(barrier, inc=1, device_id=(lax.rem(mc + j, NCHAN), mw), device_id_type=MESH)
        return carry

    lax.fori_loop(1, NWIN, greet_win, 0)
    lax.fori_loop(1, NCHAN, greet_chan, 0)

    def clear(i, carry):
        ask_ref[0, i] = 0
        return carry

    lax.fori_loop(2 * OFFS, LANES, clear, 0)

    def list_offset(h, at):
        nxt = jnp.minimum(at + 1, PAIRS - 1)
        double = jnp.logical_and(at + 1 < PAIRS, hop_ref[0, nxt] == h)
        ask_ref[0, 2 * h] = receiver_ref[0, at]
        ask_ref[0, 2 * h + 1] = receiver_ref[0, nxt]
        return jnp.minimum(at + 1 + double.astype(jnp.int32), PAIRS - 1)

    lax.fori_loop(0, OFFS, list_offset, jnp.int32(0))

    offset = offset_ref[0]
    start = jnp.minimum(offset >> 7, REC // LANES - ROWS - 1)
    shift = offset - start * LANES
    turn = lax.rem(LANES - shift, LANES)
    lane8 = lax.broadcasted_iota(jnp.int32, (CH, LANES), 1)
    keep = lane8 < LANES - shift

    def turned(r):
        return pltpu.roll(x_ref[start + r], turn, 1)

    def shift_row(r, carry):
        before, total = carry
        after = turned(r + 1)
        row = jnp.where(keep, before, after)
        seg_ref[pl.ds(pl.multiple_of(r * CH, CH), CH), :] = row
        return after, total + row

    unused, total = lax.fori_loop(
        0, ROWS, shift_row, (turned(0), jnp.zeros((CH, LANES), F32)), unroll=8
    )
    mean = jnp.sum(total, axis=1, keepdims=True) * (1.0 / NT)
    mean_ref = jnp.broadcast_to(mean, (CH, LANES))

    def centre(r, carry):
        at = pl.ds(pl.multiple_of(r * CH, CH), CH)
        seg_ref[at, :] = seg_ref[at, :] - mean_ref
        return carry

    lax.fori_loop(0, ROWS, centre, 0, unroll=8)

    pl.semaphore_wait(barrier, NWIN - 1 + NCHAN - 1)

    def ask_copy(h):
        return pltpu.make_async_remote_copy(
            src_ref=ask_ref,
            dst_ref=asked_ref.at[pl.ds(h, 1)],
            send_sem=ask_send.at[h],
            recv_sem=ask_recv.at[h],
            device_id=(lax.rem(mc + h + NCHAN - HOPS, NCHAN), mw),
            device_id_type=MESH,
        )

    def far(action):
        def run(j, carry):
            action(j + (j >= HOPS).astype(jnp.int32))
            return carry

        lax.fori_loop(0, OFFS - 1, run, 0)

    far(lambda h: ask_copy(h).start())

    for ch in range(CH):
        data = seg_ref[pl.ds(ch, ROWS, stride=CH), :] * hann_ref[...]
        part = jnp.dot(first_ref[...], data, precision=HIGH, preferred_element_type=F32)
        re, im = part[:LANES], part[LANES:]
        mixed = jnp.concatenate(
            [re * twist_ref[0] - im * twist_ref[1], re * twist_ref[1] + im * twist_ref[0]], axis=1
        )
        bins = lax.dot_general(
            second_ref[...], mixed, (((1,), (1,)), ((), ())), precision=HIGH, preferred_element_type=F32
        )
        spec_ref[0, :, ch, :] = bins[:18]
        spec_ref[1, :, ch, :] = bins[24:42]

    real, imag = spec_ref[0], spec_ref[1]
    power = real * real + imag * imag
    lane = lax.broadcasted_iota(jnp.int32, (1, CH, LANES), 2)

    def ahead(value, by):
        rolled = jnp.stack([pltpu.roll(value[r], LANES - by, 1) for r in range(value.shape[0])])
        later = jnp.concatenate([rolled[1:], rolled[-1:]], axis=0)
        return jnp.where(lane < LANES - by, rolled, later)

    window = power
    for step in (1, 2, 4, 8, 16, 32):
        window = window + ahead(window, step)
    window = window + ahead(power, 64)
    rolled = jnp.stack([pltpu.roll(window[r], HALF, 1) for r in range(BANDS + 1)])
    level = jnp.where(lane >= HALF, rolled[1:], rolled[:-1]) * (1.0 / (2 * HALF + 1))
    scale = lax.rsqrt(level + 1e-06)
    white_ref[...] = jnp.concatenate(
        [real[1 : BANDS + 1] * scale, imag[1 : BANDS + 1] * scale], axis=1
    ).astype(BF16)

    def win_copy(w, slot):
        return pltpu.make_async_remote_copy(
            src_ref=white_ref.at[w],
            dst_ref=all_ref.at[slot],
            send_sem=win_send.at[w],
            recv_sem=win_recv.at[slot],
            device_id=(mc, w),
            device_id_type=MESH,
        )

    def each_win(action):
        def run(j, carry):
            action(lax.rem(mw + j, NWIN))
            return carry

        lax.fori_loop(1, NWIN, run, 0)

    each_win(lambda w: win_copy(w, mw).start())
    all_ref[mw] = white_ref[mw]
    far(lambda h: ask_copy(h).wait_recv())
    each_win(lambda w: win_copy(w, w).wait_recv())

    by_row = jnp.dot(
        order_ref[...], all_ref[...].reshape(NWIN * 16, LANES), preferred_element_type=F32
    )
    rows_ref[...] = by_row.astype(BF16).reshape(CH, 32, LANES)

    def hop_copy(h):
        return pltpu.make_async_remote_copy(
            src_ref=send_ref.at[h],
            dst_ref=got_ref.at[h],
            send_sem=hop_send.at[h],
            recv_sem=hop_recv.at[h],
            device_id=(lax.rem(mc + NCHAN + HOPS - h, NCHAN), mw),
            device_id_type=MESH,
        )

    def hand_out(h):
        send_ref[h, 0] = rows_ref[asked_ref[h, 2 * h]]
        send_ref[h, 1] = rows_ref[asked_ref[h, 2 * h + 1]]
        hop_copy(h).start()

    far(hand_out)
    got_ref[HOPS, 0] = rows_ref[ask_ref[0, 2 * HOPS]]
    got_ref[HOPS, 1] = rows_ref[ask_ref[0, 2 * HOPS + 1]]
    far(lambda h: hop_copy(h).wait_recv())

    for q in range(PAIRS):
        h = hop_ref[0, q]
        place = (hop_ref[0, q - 1] == h).astype(jnp.int32) if q else 0
        mine = rows_ref[source_ref[0, q]].astype(F32)
        theirs = got_ref[h, place].astype(F32)
        mr, mi, tr, ti = mine[:16], mine[16:], theirs[:16], theirs[16:]
        cross_ref[0, pl.ds(q, 1), :] = jnp.sum(mr * tr + mi * ti, axis=0, keepdims=True)
        cross_ref[1, pl.ds(q, 1), :] = jnp.sum(mr * ti - mi * tr, axis=0, keepdims=True)

    column = owner_ref[...]
    up = lax.broadcasted_iota(jnp.int32, (PAIRS, PAIRS), 0)
    along = lax.broadcasted_iota(jnp.int32, (PAIRS, PAIRS), 1)
    names = jnp.sum(jnp.where(up == along, column, 0), axis=0, keepdims=True)
    slot = jnp.sum(
        jnp.where(jnp.logical_and(column == names, up < along), 1, 0), axis=0, keepdims=True
    )
    block = lax.broadcasted_iota(jnp.int32, (NCHAN, PAIRS), 0)
    for s in range(2):
        pick = jnp.where(jnp.logical_and(names == block, slot == s), 1.0, 0.0).astype(F32)
        for part in range(2):
            mail_ref[:, 2 * s + part, :] = jnp.dot(
                pick, cross_ref[part], precision=HIGH, preferred_element_type=F32
            )

    def own_copy(o, from_block):
        return pltpu.make_async_remote_copy(
            src_ref=mail_ref.at[o],
            dst_ref=out_ref.at[from_block],
            send_sem=own_send.at[o],
            recv_sem=own_recv.at[from_block],
            device_id=(o, mw),
            device_id_type=MESH,
        )

    def each_chan(action):
        def run(j, carry):
            action(lax.rem(mc + j, NCHAN))
            return carry

        lax.fori_loop(1, NCHAN, run, 0)

    each_chan(lambda o: own_copy(o, mc).start())
    out_ref[mc] = mail_ref[mc]
    each_chan(lambda o: own_copy(o, o).wait_recv())

    far(lambda h: ask_copy(h).wait_send())
    each_win(lambda w: win_copy(w, mw).wait_send())
    far(lambda h: hop_copy(h).wait_send())
    each_chan(lambda o: own_copy(o, mc).wait_send())


def local(traces, offsets, pair_source, pair_recv, pair_hop, pair_owner):
    pieces = traces.reshape(CH, REC // LANES, LANES).transpose(1, 0, 2)
    consts = [jnp.asarray(t) for t in tables()]
    smem = pl.BlockSpec(memory_space=pltpu.SMEM)
    vmem = pl.BlockSpec(memory_space=pltpu.VMEM)
    out = pl.pallas_call(
        kernel,
        out_shape=jax.ShapeDtypeStruct((NCHAN, 4, LANES), F32),
        in_specs=[smem] * 4 + [vmem] * 7,
        out_specs=vmem,
        scratch_shapes=[
            pltpu.VMEM((ROWS * CH, LANES), F32),
            pltpu.VMEM((2, BANDS + 2, CH, LANES), F32),
            pltpu.VMEM((BANDS, 16, LANES), BF16),
            pltpu.VMEM((NWIN, 16, LANES), BF16),
            pltpu.VMEM((CH, 32, LANES), BF16),
            pltpu.VMEM((OFFS, 2, 32, LANES), BF16),
            pltpu.VMEM((OFFS, 2, 32, LANES), BF16),
            pltpu.VMEM((2, PAIRS, LANES), F32),
            pltpu.VMEM((NCHAN, 4, LANES), F32),
            pltpu.SMEM((1, LANES), jnp.int32),
            pltpu.SMEM((OFFS, LANES), jnp.int32),
            pltpu.SemaphoreType.DMA((OFFS,)),
            pltpu.SemaphoreType.DMA((OFFS,)),
            pltpu.SemaphoreType.DMA((NWIN,)),
            pltpu.SemaphoreType.DMA((NWIN,)),
            pltpu.SemaphoreType.DMA((OFFS,)),
            pltpu.SemaphoreType.DMA((OFFS,)),
            pltpu.SemaphoreType.DMA((NCHAN,)),
            pltpu.SemaphoreType.DMA((NCHAN,)),
        ],
        compiler_params=pltpu.CompilerParams(collective_id=0, has_side_effects=True),
        name="cross_spectra",
    )(offsets, pair_source, pair_recv, pair_hop, pair_owner, pieces, *consts)
    return out.reshape(2 * NCHAN, 2, LANES)


def solution(mesh):
    placed = (
        P("chan", "win"),
        P("win"),
        P("chan", None),
        P("chan", None),
        P("chan", None),
        P("chan", None),
    )
    return jax.shard_map(
        local, mesh=mesh, in_specs=placed, out_specs=P("chan", None, "win"), check_vma=False
    )
```

time: 723 us -> 48.8 us (0.07)
  local copies, waits for them, and re-layouts: 238 us -> 2.8 us
  waiting for transfers between devices: 150 us -> 0 us
  matrix products: 93 us -> 0 us
  loops' own time: 84.4 us -> 0 us
  starting transfers between devices: 62.4 us -> 0 us
  other arithmetic: 54.6 us -> 0 us
  Pallas kernels: 0 us -> 44.4 us
  blocking collectives: 19.3 us -> 0 us
  between operations: 14.6 us -> 0.67 us
    unnamed x15 -> x4, local copies, waits for them, and re-layouts: 115 us -> 2.8 us
    unnamed x2 -> x0, waiting for transfers between devices: 97 us -> none
    dot_general x7 -> x0, matrix products: 93 us -> none  [the longest x1 23.2 us: transform(): jnp.dot(mixed_imag, table_sin, precision=high)]
    another operation x1 -> x0, loops' own time: 84.4 us -> none  [local(): lax.scan(advance, white, jnp.arange(1, chan_count, dtype=jnp.int32))]
    gather x130 -> x0, local copies, waits for them, and re-layouts: 80.4 us -> none  [the longest x32 20.4 us: offset_terms(): jnp.take(source_list, clipped)]
    ppermute x31 -> x0, starting transfers between devices: 62.4 us -> none  [shifted(): lax.ppermute(value, axis, [(i, (i + by) % peers) for i in range(peers)])]
    ppermute x31 -> x0, waiting for transfers between devices: 52.7 us -> none  [shifted(): lax.ppermute(value, axis, [(i, (i + by) % peers) for i in range(peers)])]
    pallas_call x0 -> x1, Pallas kernels: none -> 44.4 us  [local(): pl.pallas_call(kernel, out_shape=jax.ShapeDtypeStruct((NCHAN, 4, LANES),...]
  transfers between devices with their start and end apart: 32 -> 0, of which waited for: 32 -> 0; matrix products, arithmetic and copies ran while one was open for 14% -> 0% of each run, Pallas kernels for 0% -> 0%
where the time goes in v1:
time: 48.8 us; the launch traced here: 47.9 us
  Pallas kernels  44.4 us (91%)
  local copies, waits for them, and re-layouts  2.8 us (6%)
  between operations  0.67 us (1%)
    pallas_call x1, Pallas kernels, local(): pl.pallas_call(kernel, out_shape=jax.ShapeDtypeStruct((NCHAN, 4, LANES),...  44.4 us
    unnamed x4, local copies, waits for them, and re-layouts  2.8 us

profile of v1, /device:TPU:1, one launch (start us, length us, event | category | flops | bytes accessed | tf_op | source)
XLA Modules:
  0.0 47.9 jit_solution(16703100384620472012)
XLA Ops:
  0.7 0.0 copy-start
  0.7 0.6 %copy-done = s32[24,1]{0,1:T(1,128)S(1)} copy-done((s32[24,1]{0,1:T(1,128)S(1)}, s32[24,1]{0,1:T(1,128)}, u32[]{:S(2)}) %copy-start) | copy-done | bytes 120
  1.3 0.7 %copy.12.owner_ref = s32[24,1]{1,0:T(8,128)} copy(s32[24,1]{0,1:T(1,128)S(1)} %copy-done) | data formatting | bytes 192 | tf_op args[5]
  2.0 44.4 %cross_spectra.1 = f32[32,4,128]{2,1,0:T(4,128)} custom-call(s32[1]{0:T(128)S(6)} %copy.14.offset_ref, s32[1,24]{1,0:T(1,128)} %source_ref.1, s32[1,24]{1,0:T(1,128)} %receiver_ref.1, s32[1,24]{1,0:T(1,128)} %hop_ref.1, s32[24,1]{1,0:T(8,128)} %copy.12.owner_ref, f32[96,8,128]{2,1,0:T(8,128)} %bitcast.4, f32[256,64]{1,0:T(8,128)} %constant.10.clone.first_ref, ...), custom_call_target="tpu_custom_call" | custom-call | tf_op jit(solution)/shard_map/cross_spectra/pallas_call | solution.py:284
  46.4 1.5 %copy.15 = f32[64,2,128]{2,1,0:T(2,128)} copy(f32[64,2,128]{2,1,0:T(2,128)} %bitcast.5) | data formatting | bytes 131072
Async XLA Ops:
  0.7 0.7 %copy-start = (s32[24,1]{0,1:T(1,128)S(1)}, s32[24,1]{0,1:T(1,128)}, u32[]{:S(2)}) copy-start(s32[24,1]{0,1:T(1,128)} %param.16) | copy-start | bytes 292

commit v2 on v1

v2 whole, which is shorter than its diff:
```python
import jax
import jax.numpy as jnp
import numpy as np
from jax import lax
from jax.experimental import pallas as pl
from jax.experimental.pallas import tpu as pltpu
from jax.sharding import PartitionSpec as P

MESH = pl.DeviceIdType.MESH
NT = 8192
LANES = 128
ROWS = NT // LANES
BANDS = 16
HALF = 32
CH = 8
NWIN = 16
NCHAN = 32
HOPS = 8
OFFS = 17
PAIRS = 24
KEEP = 32
REC = 12288
F32 = jnp.float32
BF16 = jnp.bfloat16
HIGH = lax.Precision.HIGHEST


def split(value):
    high = value.astype(jnp.bfloat16)
    rest = value - high.astype(value.dtype)
    mid = rest.astype(jnp.bfloat16)
    return high, mid, (rest - mid.astype(value.dtype)).astype(jnp.bfloat16)


def tables():
    lane = np.arange(LANES)
    row = np.arange(ROWS)
    low = lane + HALF
    angle = 2.0 * np.pi / ROWS * (np.outer(low[:ROWS], row) % ROWS)
    h, m, w = split(np.concatenate([np.cos(angle), -np.sin(angle)], axis=0))
    first = np.concatenate([h, h, h, m, m, w], axis=1)
    angle = 2.0 * np.pi / NT * (np.outer(low, lane) % NT)
    twist = np.stack([np.cos(angle), -np.sin(angle)])
    band = np.arange(-1, BANDS + 1)
    angle = 2.0 * np.pi / ROWS * (np.outer(band, lane) % ROWS)
    cos, sin = np.cos(angle), np.sin(angle)
    pad = np.zeros((6, 2 * LANES))
    second = np.concatenate(
        [np.concatenate([cos, sin], axis=1), pad, np.concatenate([-sin, cos], axis=1), pad], axis=0
    )
    second = np.concatenate(split(second), axis=0)
    place = np.arange(NT).reshape(ROWS, LANES)
    hann = 0.5 - 0.5 * np.cos(2.0 * np.pi / NT * place)
    order = np.zeros((256, 256))
    for ch in range(CH):
        for part in range(2):
            for w in range(NWIN):
                order[ch * 32 + part * 16 + w, w * 16 + part * 8 + ch] = 1.0
    return (
        first.astype(jnp.bfloat16),
        twist.astype(np.float32),
        second.astype(jnp.bfloat16),
        hann.astype(np.float32),
        order.astype(jnp.bfloat16),
    )


def chan_order():
    steps = [(k, m) for k in range(4) for m in range(8) if k or m]
    return sorted(steps, key=lambda s: -(2 * min(s[0], 4 - s[0]) + min(s[1], 8 - s[1])))


def win_order():
    steps = [(i, j, k) for i in range(4) for j in range(2) for k in range(2) if i or j or k]
    return sorted(steps, key=lambda s: -(min(s[0], 4 - s[0]) + s[1] + 0.1 * s[2]))


HOP_ORDER = tuple(HOPS + d for d in (4, -4, 5, -5, 3, -3, 6, -6, 2, -2, 7, -7, 8, -8, 1, -1))


def kernel(
    offset_hbm, source_hbm, receiver_hbm, hop_hbm, owner_hbm,
    x_hbm, first_hbm, twist_hbm, second_hbm, hann_hbm, order_hbm,
    out_ref,
    offset_ref, source_ref, receiver_ref, hop_ref, owner_ref,
    x_ref, first_ref, twist_ref, second_ref, hann_ref, order_ref,
    seg_ref, spec_ref, white_ref, all_ref, rows_ref, send_ref, got_ref, cross_ref, mail_ref,
    ask_ref, asked_ref,
    in_sem, ask_send, ask_recv, win_send, win_recv, hop_send, hop_recv, own_send, own_recv, own_local,
):
    mc = lax.axis_index("chan")
    mw = lax.axis_index("win")
    chans = [
        lax.rem(mc // 8 + k, 4) * 8 + lax.rem(lax.rem(mc, 8) + m, 8) for k, m in chan_order()
    ]
    wins = [
        lax.rem(mw // 4 + i, 4) * 4 + lax.rem(lax.rem(mw, 4) // 2 + j, 2) * 2 + lax.rem(mw + k, 2)
        for i, j, k in win_order()
    ]

    barrier = pltpu.get_barrier_semaphore()
    for c in chans:
        pl.semaphore_signal(barrier, inc=1, device_id=(c, mw), device_id_type=MESH)
    for w in wins:
        pl.semaphore_signal(barrier, inc=1, device_id=(mc, w), device_id_type=MESH)

    def arrivals(ref, count, send, recv):
        part = ref.at[pl.ds(0, count)]
        return pltpu.make_async_remote_copy(
            src_ref=part, dst_ref=part, send_sem=send, recv_sem=recv, device_id=(mc, mw), device_id_type=MESH
        )

    asks = arrivals(asked_ref, OFFS - 1, ask_send, ask_recv)
    windows = arrivals(all_ref, NWIN - 1, win_send, win_recv)
    hops = arrivals(got_ref, OFFS - 1, hop_send, hop_recv)
    owns = arrivals(mail_ref, NCHAN - 1, own_send, own_recv)

    operands = (
        (offset_hbm, offset_ref), (x_hbm, x_ref), (receiver_hbm, receiver_ref), (hop_hbm, hop_ref),
        (hann_hbm, hann_ref), (first_hbm, first_ref), (twist_hbm, twist_ref), (second_hbm, second_ref),
        (order_hbm, order_ref), (source_hbm, source_ref), (owner_hbm, owner_ref),
    )
    loads = [pltpu.make_async_copy(src, dst, in_sem.at[i]) for i, (src, dst) in enumerate(operands)]
    for load in loads:
        load.start()

    def clear(i, carry):
        ask_ref[0, i] = 0
        return carry

    lax.fori_loop(2 * OFFS, LANES, clear, 0)

    def list_offset(h, at):
        nxt = jnp.minimum(at + 1, PAIRS - 1)
        double = jnp.logical_and(at + 1 < PAIRS, hop_ref[0, nxt] == h)
        ask_ref[0, 2 * h] = receiver_ref[0, at]
        ask_ref[0, 2 * h + 1] = receiver_ref[0, nxt]
        return jnp.minimum(at + 1 + double.astype(jnp.int32), PAIRS - 1)

    loads[2].wait()
    loads[3].wait()
    lax.fori_loop(0, OFFS, list_offset, jnp.int32(0))

    loads[0].wait()
    loads[1].wait()
    offset = offset_ref[0]
    start = jnp.minimum(offset >> 7, REC // LANES - ROWS - 1)
    shift = offset - start * LANES
    turn = lax.rem(LANES - shift, LANES)
    lane8 = lax.broadcasted_iota(jnp.int32, (CH, LANES), 1)
    keep = lane8 < LANES - shift

    def turned(r):
        return pltpu.roll(x_ref[start + r], turn, 1)

    def shift_row(r, carry):
        before, total = carry
        after = turned(r + 1)
        row = jnp.where(keep, before, after)
        seg_ref[pl.ds(pl.multiple_of(r * CH, CH), CH), :] = row
        return after, total + row

    unused, total = lax.fori_loop(
        0, ROWS, shift_row, (turned(0), jnp.zeros((CH, LANES), F32)), unroll=8
    )
    mean = jnp.sum(total, axis=1, keepdims=True) * (1.0 / NT)
    mean_ref = jnp.broadcast_to(mean, (CH, LANES))

    def centre(r, carry):
        at = pl.ds(pl.multiple_of(r * CH, CH), CH)
        seg_ref[at, :] = seg_ref[at, :] - mean_ref
        return carry

    lax.fori_loop(0, ROWS, centre, 0, unroll=8)

    pl.semaphore_wait(barrier, NWIN - 1 + NCHAN - 1)

    def ask_copy(h):
        return pltpu.make_async_remote_copy(
            src_ref=ask_ref,
            dst_ref=asked_ref.at[pl.ds(h, 1)],
            send_sem=ask_send,
            recv_sem=ask_recv,
            device_id=(lax.rem(mc + h + NCHAN - HOPS, NCHAN), mw),
            device_id_type=MESH,
        )

    for h in HOP_ORDER:
        ask_copy(h).start()
    for load in loads[4:]:
        load.wait()

    data = jnp.concatenate(
        [seg_ref[pl.ds(ch, ROWS, stride=CH), :] * hann_ref[...] for ch in range(CH)], axis=1
    )
    high, mid, low = split(data)
    part = jnp.dot(
        first_ref[...],
        jnp.concatenate([high, mid, low, high, mid, high], axis=0),
        preferred_element_type=F32,
    )
    terms = []
    for ch in range(CH):
        at = slice(ch * LANES, (ch + 1) * LANES)
        re = jnp.concatenate([part[:ROWS, at]] * 2, axis=0)
        im = jnp.concatenate([part[ROWS:, at]] * 2, axis=0)
        terms.append(
            split(
                jnp.concatenate(
                    [re * twist_ref[0] - im * twist_ref[1], re * twist_ref[1] + im * twist_ref[0]],
                    axis=1,
                )
            )
        )
    high, mid, low = (jnp.concatenate([t[i] for t in terms], axis=0) for i in range(3))

    def across(rows, value):
        return lax.dot_general(
            second_ref[pl.ds(0, rows), :],
            value,
            (((1,), (1,)), ((), ())),
            preferred_element_type=F32,
        )

    one, two, three = across(144, high), across(96, mid), across(48, low)
    bins = one[:48] + ((one[48:96] + two[:48]) + ((one[96:] + two[48:]) + three))
    for ch in range(CH):
        at = slice(ch * LANES, (ch + 1) * LANES)
        spec_ref[0, :, ch, :] = bins[:18, at]
        spec_ref[1, :, ch, :] = bins[24:42, at]

    real, imag = spec_ref[0], spec_ref[1]
    power = real * real + imag * imag
    lane = lax.broadcasted_iota(jnp.int32, (1, CH, LANES), 2)

    def ahead(value, by):
        rolled = jnp.stack([pltpu.roll(value[r], LANES - by, 1) for r in range(value.shape[0])])
        later = jnp.concatenate([rolled[1:], rolled[-1:]], axis=0)
        return jnp.where(lane < LANES - by, rolled, later)

    window = power
    for step in (1, 2, 4, 8, 16, 32):
        window = window + ahead(window, step)
    window = window + ahead(power, 64)
    rolled = jnp.stack([pltpu.roll(window[r], HALF, 1) for r in range(BANDS + 1)])
    level = jnp.where(lane >= HALF, rolled[1:], rolled[:-1]) * (1.0 / (2 * HALF + 1))
    scale = lax.rsqrt(level + 1e-06)
    white_ref[...] = jnp.concatenate(
        [real[1 : BANDS + 1] * scale, imag[1 : BANDS + 1] * scale], axis=1
    ).astype(BF16)

    def win_copy(w, slot):
        return pltpu.make_async_remote_copy(
            src_ref=white_ref.at[w],
            dst_ref=all_ref.at[slot],
            send_sem=win_send,
            recv_sem=win_recv,
            device_id=(mc, w),
            device_id_type=MESH,
        )

    for w in wins:
        win_copy(w, mw).start()

    all_ref[mw] = white_ref[mw]
    asks.wait_recv()
    windows.wait_recv()

    by_row = jnp.dot(
        order_ref[...], all_ref[...].reshape(NWIN * 16, LANES), preferred_element_type=F32
    )
    rows_ref[...] = by_row.astype(BF16).reshape(CH, 32, LANES)

    def hop_copy(h):
        return pltpu.make_async_remote_copy(
            src_ref=send_ref.at[h],
            dst_ref=got_ref.at[h],
            send_sem=hop_send,
            recv_sem=hop_recv,
            device_id=(lax.rem(mc + NCHAN + HOPS - h, NCHAN), mw),
            device_id_type=MESH,
        )

    def hand_out(h):
        send_ref[h, 0] = rows_ref[asked_ref[h, 2 * h]]
        send_ref[h, 1] = rows_ref[asked_ref[h, 2 * h + 1]]
        hop_copy(h).start()

    for h in HOP_ORDER:
        hand_out(h)

    got_ref[HOPS, 0] = rows_ref[ask_ref[0, 2 * HOPS]]
    got_ref[HOPS, 1] = rows_ref[ask_ref[0, 2 * HOPS + 1]]
    names = owner_ref[...]
    up = lax.broadcasted_iota(jnp.int32, (PAIRS, PAIRS), 0)
    along = lax.broadcasted_iota(jnp.int32, (PAIRS, PAIRS), 1)
    column = jnp.sum(jnp.where(up == along, names, 0), axis=1, keepdims=True)
    slot = jnp.sum(
        jnp.where(jnp.logical_and(column == names, up < along), 1, 0), axis=0, keepdims=True
    )
    block = lax.broadcasted_iota(jnp.int32, (2 * NCHAN, PAIRS), 0)
    place = names + slot * NCHAN
    chosen = jnp.where(place == block, 1.0, 0.0).astype(F32)
    chosen = jnp.concatenate([chosen, jnp.zeros((2 * NCHAN, KEEP - PAIRS), F32)], axis=1)
    pick = jnp.concatenate([chosen] * 3, axis=1).astype(BF16)
    cross_ref[pl.ds(PAIRS, KEEP - PAIRS), :] = jnp.zeros((KEEP - PAIRS, 2 * LANES), F32)

    hops.wait_recv()

    for q in range(PAIRS):
        h = hop_ref[0, q]
        place = (hop_ref[0, q - 1] == h).astype(jnp.int32) if q else 0
        mine = rows_ref[source_ref[0, q]].astype(F32)
        theirs = got_ref[h, place].astype(F32)
        mr, mi, tr, ti = mine[:16], mine[16:], theirs[:16], theirs[16:]
        cross_ref[pl.ds(q, 1), pl.ds(0, LANES)] = jnp.sum(mr * tr + mi * ti, axis=0, keepdims=True)
        cross_ref[pl.ds(q, 1), pl.ds(LANES, LANES)] = jnp.sum(mr * ti - mi * tr, axis=0, keepdims=True)

    high, mid, low = split(cross_ref[...])
    mail = jnp.dot(pick, jnp.concatenate([high, mid, low], axis=0), preferred_element_type=F32)
    for s in range(2):
        for part in range(2):
            mail_ref[:, 2 * s + part, :] = mail[s * NCHAN : (s + 1) * NCHAN, part * LANES : (part + 1) * LANES]

    def own_copy(o, from_block):
        return pltpu.make_async_remote_copy(
            src_ref=mail_ref.at[o],
            dst_ref=out_ref.at[from_block],
            send_sem=own_send,
            recv_sem=own_recv,
            device_id=(o, mw),
            device_id_type=MESH,
        )

    for o in chans:
        own_copy(o, mc).start()

    keep_own = pltpu.make_async_copy(mail_ref.at[mc], out_ref.at[mc], own_local)
    keep_own.start()
    asks.wait_send()
    windows.wait_send()
    hops.wait_send()
    keep_own.wait()
    owns.wait_send()
    owns.wait_recv()


def local(traces, offsets, pair_source, pair_recv, pair_hop, pair_owner):
    pieces = traces.reshape(CH, REC // LANES, LANES).transpose(1, 0, 2)
    consts = [jnp.asarray(t) for t in tables()]
    anywhere = pl.BlockSpec(memory_space=pl.ANY)
    row = (1, PAIRS)
    out = pl.pallas_call(
        kernel,
        out_shape=jax.ShapeDtypeStruct((NCHAN, 4, LANES), F32),
        in_specs=[anywhere] * 11,
        out_specs=anywhere,
        scratch_shapes=[
            pltpu.SMEM((1,), jnp.int32),
            pltpu.SMEM(row, jnp.int32),
            pltpu.SMEM(row, jnp.int32),
            pltpu.SMEM(row, jnp.int32),
            pltpu.VMEM(row, jnp.int32),
            pltpu.VMEM((REC // LANES, CH, LANES), F32),
        ]
        + [pltpu.VMEM(c.shape, c.dtype) for c in consts]
        + [
            pltpu.VMEM((ROWS * CH, LANES), F32),
            pltpu.VMEM((2, BANDS + 2, CH, LANES), F32),
            pltpu.VMEM((BANDS, 16, LANES), BF16),
            pltpu.VMEM((NWIN, 16, LANES), BF16),
            pltpu.VMEM((CH, 32, LANES), BF16),
            pltpu.VMEM((OFFS, 2, 32, LANES), BF16),
            pltpu.VMEM((OFFS, 2, 32, LANES), BF16),
            pltpu.VMEM((KEEP, 2 * LANES), F32),
            pltpu.VMEM((NCHAN, 4, LANES), F32),
            pltpu.SMEM((1, LANES), jnp.int32),
            pltpu.SMEM((OFFS, LANES), jnp.int32),
            pltpu.SemaphoreType.DMA((11,)),
        ]
        + [pltpu.SemaphoreType.DMA] * 9,
        compiler_params=pltpu.CompilerParams(collective_id=0, has_side_effects=True),
        name="cross_spectra",
    )(offsets, pair_source, pair_recv, pair_hop, pair_owner.reshape(row), pieces, *consts)
    return out.reshape(2 * NCHAN, 2, LANES)


def solution(mesh):
    placed = (
        P("chan", "win"),
        P("win"),
        P("chan", None),
        P("chan", None),
        P("chan", None),
        P("chan", None),
    )
    return jax.shard_map(
        local, mesh=mesh, in_specs=placed, out_specs=P("chan", None, "win"), check_vma=False
    )
```

time: 48.8 us -> 39.4 us (0.81)
  Pallas kernels: 44.4 us -> 36.8 us
  local copies, waits for them, and re-layouts: 2.8 us -> 1.47 us
    pallas_call x1, Pallas kernels: 44.4 us -> 36.8 us  [local(): pl.pallas_call(kernel, out_shape=jax.ShapeDtypeStruct((NCHAN, 4, LANES),...]
    unnamed x4 -> x1, local copies, waits for them, and re-layouts: 2.8 us -> 1.47 us
where the time goes in v2:
time: 39.4 us; the launch traced here: 38.9 us
  Pallas kernels  36.8 us (93%)
  local copies, waits for them, and re-layouts  1.47 us (4%)
  between operations  0.66 us (2%)
    pallas_call x1, Pallas kernels, local(): pl.pallas_call(kernel, out_shape=jax.ShapeDtypeStruct((NCHAN, 4, LANES),...  36.8 us
    unnamed x1, local copies, waits for them, and re-layouts  1.47 us

profile of v2, /device:TPU:1, one launch (start us, length us, event | category | flops | bytes accessed | tf_op | source)
XLA Modules:
  0.0 38.9 jit_solution(18063275329804665108)
XLA Ops:
  0.7 36.8 %cross_spectra.1 = f32[32,4,128]{2,1,0:T(4,128)} custom-call(s32[1]{0:T(128)S(6)} %copy.13.offset_hbm, s32[1,24]{1,0:T(1,128)} %source_hbm.1, s32[1,24]{1,0:T(1,128)} %receiver_hbm.1, s32[1,24]{1,0:T(1,128)} %hop_hbm.1, s32[1,24]{1,0:T(1,128)} %bitcast.7, f32[96,8,128]{2,1,0:T(8,128)} %bitcast.5, bf16[128,384]{1,0:T(8,128)(2,1)} %constant.10.clone.first_hbm, ...), custom_call_target="tpu_custom_call" | custom-call | tf_op jit(solution)/shard_map/cross_spectra/pallas_call | solution.py:353
  37.4 1.5 %copy.14 = f32[64,2,128]{2,1,0:T(2,128)} copy(f32[64,2,128]{2,1,0:T(2,128)} %bitcast.6) | data formatting | bytes 131072

commit v3 on v2

--- a/solution.py
+++ b/solution.py
@@ -98,12 +98,24 @@
         for i, j, k in win_order()
     ]
 
+    operands = (
+        (x_hbm, x_ref), (offset_hbm, offset_ref), (hann_hbm, hann_ref), (first_hbm, first_ref),
+        (twist_hbm, twist_ref), (second_hbm, second_ref),
+        (receiver_hbm, receiver_ref), (hop_hbm, hop_ref), (order_hbm, order_ref), (source_hbm, source_ref), (owner_hbm, owner_ref),
+    )
+    loads = [pltpu.make_async_copy(src, dst, in_sem.at[i]) for i, (src, dst) in enumerate(operands)]
+    for load in loads[:6]:
+        load.start()
+
     barrier = pltpu.get_barrier_semaphore()
     for c in chans:
         pl.semaphore_signal(barrier, inc=1, device_id=(c, mw), device_id_type=MESH)
     for w in wins:
         pl.semaphore_signal(barrier, inc=1, device_id=(mc, w), device_id_type=MESH)
 
+    for load in loads[6:]:
+        load.start()
+
     def arrivals(ref, count, send, recv):
         part = ref.at[pl.ds(0, count)]
         return pltpu.make_async_remote_copy(
@@ -114,32 +126,6 @@
     windows = arrivals(all_ref, NWIN - 1, win_send, win_recv)
     hops = arrivals(got_ref, OFFS - 1, hop_send, hop_recv)
     owns = arrivals(mail_ref, NCHAN - 1, own_send, own_recv)
-
-    operands = (
-        (offset_hbm, offset_ref), (x_hbm, x_ref), (receiver_hbm, receiver_ref), (hop_hbm, hop_ref),
-        (hann_hbm, hann_ref), (first_hbm, first_ref), (twist_hbm, twist_ref), (second_hbm, second_ref),
-        (order_hbm, order_ref), (source_hbm, source_ref), (owner_hbm, owner_ref),
-    )
-    loads = [pltpu.make_async_copy(src, dst, in_sem.at[i]) for i, (src, dst) in enumerate(operands)]
-    for load in loads:
-        load.start()
-
-    def clear(i, carry):
-        ask_ref[0, i] = 0
-        return carry
-
-    lax.fori_loop(2 * OFFS, LANES, clear, 0)
-
-    def list_offset(h, at):
-        nxt = jnp.minimum(at + 1, PAIRS - 1)
-        double = jnp.logical_and(at + 1 < PAIRS, hop_ref[0, nxt] == h)
-        ask_ref[0, 2 * h] = receiver_ref[0, at]
-        ask_ref[0, 2 * h + 1] = receiver_ref[0, nxt]
-        return jnp.minimum(at + 1 + double.astype(jnp.int32), PAIRS - 1)
-
-    loads[2].wait()
-    loads[3].wait()
-    lax.fori_loop(0, OFFS, list_offset, jnp.int32(0))
 
     loads[0].wait()
     loads[1].wait()
@@ -173,8 +159,6 @@
 
     lax.fori_loop(0, ROWS, centre, 0, unroll=8)
 
-    pl.semaphore_wait(barrier, NWIN - 1 + NCHAN - 1)
-
     def ask_copy(h):
         return pltpu.make_async_remote_copy(
             src_ref=ask_ref,
@@ -185,11 +169,9 @@
             device_id_type=MESH,
         )
 
-    for h in HOP_ORDER:
-        ask_copy(h).start()
-    for load in loads[4:]:
+
+    for load in loads[2:6]:
         load.wait()
-
     data = jnp.concatenate(
         [seg_ref[pl.ds(ch, ROWS, stride=CH), :] * hann_ref[...] for ch in range(CH)], axis=1
     )
@@ -259,17 +241,39 @@
             device_id_type=MESH,
         )
 
+    def clear(i, carry):
+        ask_ref[0, i] = 0
+        return carry
+
+    lax.fori_loop(2 * OFFS, LANES, clear, 0)
+
+    def list_offset(h, at):
+        nxt = jnp.minimum(at + 1, PAIRS - 1)
+        double = jnp.logical_and(at + 1 < PAIRS, hop_ref[0, nxt] == h)
+        ask_ref[0, 2 * h] = receiver_ref[0, at]
+        ask_ref[0, 2 * h + 1] = receiver_ref[0, nxt]
+        return jnp.minimum(at + 1 + double.astype(jnp.int32), PAIRS - 1)
+
+    loads[6].wait()
+    loads[7].wait()
+    lax.fori_loop(0, OFFS, list_offset, jnp.int32(0))
+
+    pl.semaphore_wait(barrier, NWIN - 1 + NCHAN - 1)
+    for h in HOP_ORDER:
+        ask_copy(h).start()
     for w in wins:
         win_copy(w, mw).start()
 
     all_ref[mw] = white_ref[mw]
-    asks.wait_recv()
     windows.wait_recv()
 
+    for load in loads[8:]:
+        load.wait()
     by_row = jnp.dot(
         order_ref[...], all_ref[...].reshape(NWIN * 16, LANES), preferred_element_type=F32
     )
     rows_ref[...] = by_row.astype(BF16).reshape(CH, 32, LANES)
+    asks.wait_recv()
 
     def hop_copy(h):
         return pltpu.make_async_remote_copy(
@@ -352,7 +356,7 @@
     row = (1, PAIRS)
     out = pl.pallas_call(
         kernel,
-        out_shape=jax.ShapeDtypeStruct((NCHAN, 4, LANES), F32),
+        out_shape=pltpu.VMEM((NCHAN, 4, LANES), F32),
         in_specs=[anywhere] * 11,
         out_specs=anywhere,
         scratch_shapes=[

time: 39.4 us -> 37.1 us (0.942)
  Pallas kernels: 36.8 us -> 35.7 us
  local copies, waits for them, and re-layouts: 1.47 us -> 0.63 us
    pallas_call x1, Pallas kernels: 36.8 us -> 35.7 us  [local(): pl.pallas_call(kernel, out_shape=pltpu.VMEM((NCHAN, 4, LANES), F32), in_s...]
    unnamed x1, local copies, waits for them, and re-layouts: 1.47 us -> 0.63 us
where the time goes in v3:
time: 37.1 us; the launch traced here: 37 us
  Pallas kernels  35.7 us (96%)
  between operations  0.66 us (2%)
  local copies, waits for them, and re-layouts  0.63 us (2%)
    pallas_call x1, Pallas kernels, local(): pl.pallas_call(kernel, out_shape=pltpu.VMEM((NCHAN, 4, LANES), F32), in_s...  35.7 us

profile of v3, /device:TPU:1, one launch (start us, length us, event | category | flops | bytes accessed | tf_op | source)
XLA Modules:
  0.0 37.0 jit_solution(14373967223339749910)
XLA Ops:
  0.7 35.7 %cross_spectra.1 = f32[32,4,128]{2,1,0:T(4,128)S(1)} custom-call(s32[1]{0:T(128)S(6)} %copy.14.offset_hbm, s32[1,24]{1,0:T(1,128)} %source_hbm.1, s32[1,24]{1,0:T(1,128)} %receiver_hbm.1, s32[1,24]{1,0:T(1,128)} %hop_hbm.1, s32[1,24]{1,0:T(1,128)} %bitcast.7, f32[96,8,128]{2,1,0:T(8,128)} %bitcast.6, bf16[128,384]{1,0:T(8,128)(2,1)} %constant.10.clone.first_hbm, ...), custom_call_target="tpu_custom_call" | custom-call | tf_op jit(solution)/shard_map/cross_spectra/pallas_call | solution.py:357
  36.3 0.6 %copy.13 = f32[64,2,128]{2,1,0:T(2,128)} copy(f32[64,2,128]{2,1,0:T(2,128)S(1)} %bitcast.5) | data formatting | bytes 131072

commit v4 on v3

--- a/solution.py
+++ b/solution.py
@@ -18,7 +18,9 @@
 HOPS = 8
 OFFS = 17
 PAIRS = 24
-KEEP = 32
+KEEP = 48
+GROUPS = 4
+SHARE = 4
 REC = 12288
 F32 = jnp.float32
 BF16 = jnp.bfloat16
@@ -82,10 +84,10 @@
     offset_hbm, source_hbm, receiver_hbm, hop_hbm, owner_hbm,
     x_hbm, first_hbm, twist_hbm, second_hbm, hann_hbm, order_hbm,
     out_ref,
-    offset_ref, source_ref, receiver_ref, hop_ref, owner_ref,
+    offset_ref, source_ref, receiver_ref, hop_ref, owner_ref, hops_ref,
     x_ref, first_ref, twist_ref, second_ref, hann_ref, order_ref,
     seg_ref, spec_ref, white_ref, all_ref, rows_ref, send_ref, got_ref, cross_ref, mail_ref,
-    ask_ref, asked_ref,
+    ask_ref, asked_ref, mine_ref,
     in_sem, ask_send, ask_recv, win_send, win_recv, hop_send, hop_recv, own_send, own_recv, own_local,
 ):
     mc = lax.axis_index("chan")
@@ -101,19 +103,17 @@
     operands = (
         (x_hbm, x_ref), (offset_hbm, offset_ref), (hann_hbm, hann_ref), (first_hbm, first_ref),
         (twist_hbm, twist_ref), (second_hbm, second_ref),
-        (receiver_hbm, receiver_ref), (hop_hbm, hop_ref), (order_hbm, order_ref), (source_hbm, source_ref), (owner_hbm, owner_ref),
+        (receiver_hbm, receiver_ref), (hop_hbm, hop_ref), (source_hbm, source_ref), (order_hbm, order_ref), (owner_hbm, owner_ref), (hop_hbm, hops_ref),
     )
     loads = [pltpu.make_async_copy(src, dst, in_sem.at[i]) for i, (src, dst) in enumerate(operands)]
-    for load in loads[:6]:
-        load.start()
-
     barrier = pltpu.get_barrier_semaphore()
-    for c in chans:
-        pl.semaphore_signal(barrier, inc=1, device_id=(c, mw), device_id_type=MESH)
+    for d in HOP_ORDER:
+        near = lax.rem(mc + d + NCHAN - HOPS, NCHAN)
+        pl.semaphore_signal(barrier, inc=1, device_id=(near, mw), device_id_type=MESH)
     for w in wins:
         pl.semaphore_signal(barrier, inc=1, device_id=(mc, w), device_id_type=MESH)
 
-    for load in loads[6:]:
+    for load in loads:
         load.start()
 
     def arrivals(ref, count, send, recv):
@@ -124,7 +124,7 @@
 
     asks = arrivals(asked_ref, OFFS - 1, ask_send, ask_recv)
     windows = arrivals(all_ref, NWIN - 1, win_send, win_recv)
-    hops = arrivals(got_ref, OFFS - 1, hop_send, hop_recv)
+    hops = arrivals(got_ref, OFFS - 1, hop_send, hop_recv.at[0])
     owns = arrivals(mail_ref, NCHAN - 1, own_send, own_recv)
 
     loads[0].wait()
@@ -251,14 +251,16 @@
         nxt = jnp.minimum(at + 1, PAIRS - 1)
         double = jnp.logical_and(at + 1 < PAIRS, hop_ref[0, nxt] == h)
         ask_ref[0, 2 * h] = receiver_ref[0, at]
+        mine_ref[0, 2 * h] = source_ref[0, at]
+        mine_ref[0, 2 * h + 1] = source_ref[0, nxt]
         ask_ref[0, 2 * h + 1] = receiver_ref[0, nxt]
         return jnp.minimum(at + 1 + double.astype(jnp.int32), PAIRS - 1)
 
-    loads[6].wait()
-    loads[7].wait()
+    for load in loads[6:9]:
+        load.wait()
     lax.fori_loop(0, OFFS, list_offset, jnp.int32(0))
 
-    pl.semaphore_wait(barrier, NWIN - 1 + NCHAN - 1)
+    pl.semaphore_wait(barrier, NWIN - 1 + OFFS - 1)
     for h in HOP_ORDER:
         ask_copy(h).start()
     for w in wins:
@@ -267,7 +269,7 @@
     all_ref[mw] = white_ref[mw]
     windows.wait_recv()
 
-    for load in loads[8:]:
+    for load in loads[9:]:
         load.wait()
     by_row = jnp.dot(
         order_ref[...], all_ref[...].reshape(NWIN * 16, LANES), preferred_element_type=F32
@@ -280,7 +282,7 @@
             src_ref=send_ref.at[h],
             dst_ref=got_ref.at[h],
             send_sem=hop_send,
-            recv_sem=hop_recv,
+            recv_sem=hop_recv.at[HOP_ORDER.index(h) // SHARE],
             device_id=(lax.rem(mc + NCHAN + HOPS - h, NCHAN), mw),
             device_id_type=MESH,
         )
@@ -296,29 +298,42 @@
     got_ref[HOPS, 0] = rows_ref[ask_ref[0, 2 * HOPS]]
     got_ref[HOPS, 1] = rows_ref[ask_ref[0, 2 * HOPS + 1]]
     names = owner_ref[...]
+    offs = hops_ref[...]
     up = lax.broadcasted_iota(jnp.int32, (PAIRS, PAIRS), 0)
     along = lax.broadcasted_iota(jnp.int32, (PAIRS, PAIRS), 1)
-    column = jnp.sum(jnp.where(up == along, names, 0), axis=1, keepdims=True)
-    slot = jnp.sum(
-        jnp.where(jnp.logical_and(column == names, up < along), 1, 0), axis=0, keepdims=True
-    )
-    block = lax.broadcasted_iota(jnp.int32, (2 * NCHAN, PAIRS), 0)
-    place = names + slot * NCHAN
-    chosen = jnp.where(place == block, 1.0, 0.0).astype(F32)
-    chosen = jnp.concatenate([chosen, jnp.zeros((2 * NCHAN, KEEP - PAIRS), F32)], axis=1)
+
+    def upright(row):
+        return jnp.sum(jnp.where(up == along, row, 0), axis=1, keepdims=True)
+
+    def rank(column, row):
+        return jnp.sum(
+            jnp.where(jnp.logical_and(column == row, along < up), 1, 0), axis=1, keepdims=True
+        )
+
+    name, off = upright(names), upright(offs)
+    target = name + rank(name, names) * NCHAN + 1
+    place = off * 2 + rank(off, offs)
+    spot = lax.broadcasted_iota(jnp.int32, (PAIRS, KEEP), 1)
+    wanted = jnp.sum(jnp.where(place == spot, target, 0), axis=0, keepdims=True) - 1
+    block = lax.broadcasted_iota(jnp.int32, (2 * NCHAN, KEEP), 0)
+    chosen = jnp.where(wanted == block, 1.0, 0.0).astype(F32)
     pick = jnp.concatenate([chosen] * 3, axis=1).astype(BF16)
-    cross_ref[pl.ds(PAIRS, KEEP - PAIRS), :] = jnp.zeros((KEEP - PAIRS, 2 * LANES), F32)
-
-    hops.wait_recv()
-
-    for q in range(PAIRS):
-        h = hop_ref[0, q]
-        place = (hop_ref[0, q - 1] == h).astype(jnp.int32) if q else 0
-        mine = rows_ref[source_ref[0, q]].astype(F32)
-        theirs = got_ref[h, place].astype(F32)
-        mr, mi, tr, ti = mine[:16], mine[16:], theirs[:16], theirs[16:]
-        cross_ref[pl.ds(q, 1), pl.ds(0, LANES)] = jnp.sum(mr * tr + mi * ti, axis=0, keepdims=True)
-        cross_ref[pl.ds(q, 1), pl.ds(LANES, LANES)] = jnp.sum(mr * ti - mi * tr, axis=0, keepdims=True)
+    cross_ref[pl.ds(32, KEEP - 32), :] = jnp.zeros((KEEP - 32, 2 * LANES), F32)
+
+    def cross(h):
+        for i in range(2):
+            mine = rows_ref[mine_ref[0, 2 * h + i]].astype(F32)
+            theirs = got_ref[h, i].astype(F32)
+            mr, mi, tr, ti = mine[:16], mine[16:], theirs[:16], theirs[16:]
+            at = pl.ds(2 * h + i, 1)
+            cross_ref[at, pl.ds(0, LANES)] = jnp.sum(mr * tr + mi * ti, axis=0, keepdims=True)
+            cross_ref[at, pl.ds(LANES, LANES)] = jnp.sum(mr * ti - mi * tr, axis=0, keepdims=True)
+
+    cross(HOPS)
+    for g in range(GROUPS):
+        arrivals(got_ref, SHARE, hop_send, hop_recv.at[g]).wait_recv()
+        for h in HOP_ORDER[g * SHARE : (g + 1) * SHARE]:
+            cross(h)
 
     high, mid, low = split(cross_ref[...])
     mail = jnp.dot(pick, jnp.concatenate([high, mid, low], axis=0), preferred_element_type=F32)
@@ -365,6 +380,7 @@
             pltpu.SMEM(row, jnp.int32),
             pltpu.SMEM(row, jnp.int32),
             pltpu.VMEM(row, jnp.int32),
+            pltpu.VMEM(row, jnp.int32),
             pltpu.VMEM((REC // LANES, CH, LANES), F32),
         ]
         + [pltpu.VMEM(c.shape, c.dtype) for c in consts]
@@ -380,9 +396,12 @@
             pltpu.VMEM((NCHAN, 4, LANES), F32),
             pltpu.SMEM((1, LANES), jnp.int32),
             pltpu.SMEM((OFFS, LANES), jnp.int32),
-            pltpu.SemaphoreType.DMA((11,)),
+            pltpu.SMEM((1, LANES), jnp.int32),
+            pltpu.SemaphoreType.DMA((12,)),
         ]
-        + [pltpu.SemaphoreType.DMA] * 9,
+        + [pltpu.SemaphoreType.DMA] * 5
+        + [pltpu.SemaphoreType.DMA((GROUPS,))]
+        + [pltpu.SemaphoreType.DMA] * 3,
         compiler_params=pltpu.CompilerParams(collective_id=0, has_side_effects=True),
         name="cross_spectra",
     )(offsets, pair_source, pair_recv, pair_hop, pair_owner.reshape(row), pieces, *consts)

time: 37.1 us -> 36.3 us (0.978)
  Pallas kernels: 35.7 us -> 34.9 us
    pallas_call x1, Pallas kernels: 35.7 us -> 34.9 us  [local(): pl.pallas_call(kernel, out_shape=pltpu.VMEM((NCHAN, 4, LANES), F32), in_s...]
where the time goes in v4:
time: 36.3 us; the launch traced here: 36.2 us
  Pallas kernels  34.9 us (96%)
  between operations  0.66 us (2%)
  local copies, waits for them, and re-layouts  0.63 us (2%)
    pallas_call x1, Pallas kernels, local(): pl.pallas_call(kernel, out_shape=pltpu.VMEM((NCHAN, 4, LANES), F32), in_s...  34.9 us

profile of v4, /device:TPU:1, one launch (start us, length us, event | category | flops | bytes accessed | tf_op | source)
XLA Modules:
  0.0 36.2 jit_solution(2416916488852391555)
XLA Ops:
  0.7 34.9 %cross_spectra.1 = f32[32,4,128]{2,1,0:T(4,128)S(1)} custom-call(s32[1]{0:T(128)S(6)} %copy.14.offset_hbm, s32[1,24]{1,0:T(1,128)} %source_hbm.1, s32[1,24]{1,0:T(1,128)} %receiver_hbm.1, s32[1,24]{1,0:T(1,128)} %hop_hbm.1, s32[1,24]{1,0:T(1,128)} %bitcast.7, f32[96,8,128]{2,1,0:T(8,128)} %bitcast.6, bf16[128,384]{1,0:T(8,128)(2,1)} %constant.10.clone.first_hbm, ...), custom_call_target="tpu_custom_call" | custom-call | tf_op jit(solution)/shard_map/cross_spectra/pallas_call | solution.py:372
  35.5 0.6 %copy.13 = f32[64,2,128]{2,1,0:T(2,128)} copy(f32[64,2,128]{2,1,0:T(2,128)S(1)} %bitcast.5) | data formatting | bytes 131072

commit v5 on v4

--- a/solution.py
+++ b/solution.py
@@ -19,8 +19,8 @@
 OFFS = 17
 PAIRS = 24
 KEEP = 48
-GROUPS = 4
-SHARE = 4
+GROUPS = 8
+SHARE = 2
 REC = 12288
 F32 = jnp.float32
 BF16 = jnp.bfloat16
@@ -67,11 +67,6 @@
     )
 
 
-def chan_order():
-    steps = [(k, m) for k in range(4) for m in range(8) if k or m]
-    return sorted(steps, key=lambda s: -(2 * min(s[0], 4 - s[0]) + min(s[1], 8 - s[1])))
-
-
 def win_order():
     steps = [(i, j, k) for i in range(4) for j in range(2) for k in range(2) if i or j or k]
     return sorted(steps, key=lambda s: -(min(s[0], 4 - s[0]) + s[1] + 0.1 * s[2]))
@@ -92,9 +87,6 @@
 ):
     mc = lax.axis_index("chan")
     mw = lax.axis_index("win")
-    chans = [
-        lax.rem(mc // 8 + k, 4) * 8 + lax.rem(lax.rem(mc, 8) + m, 8) for k, m in chan_order()
-    ]
     wins = [
         lax.rem(mw // 4 + i, 4) * 4 + lax.rem(lax.rem(mw, 4) // 2 + j, 2) * 2 + lax.rem(mw + k, 2)
         for i, j, k in win_order()
@@ -351,8 +343,12 @@
             device_id_type=MESH,
         )
 
-    for o in chans:
-        own_copy(o, mc).start()
+    for j in range(NCHAN):
+        o = lax.rem(mc // 8 + 2 + j, 4) * 8 + j // 4
+
+        @pl.when(o != mc)
+        def _(o=o):
+            own_copy(o, mc).start()
 
     keep_own = pltpu.make_async_copy(mail_ref.at[mc], out_ref.at[mc], own_local)
     keep_own.start()

time: 36.3 us -> 36.3 us (level)
  no operation moved by 1% of the time
where the time goes in v5:
time: 36.3 us; the launch traced here: 36.2 us
  Pallas kernels  34.9 us (96%)
  between operations  0.66 us (2%)
  local copies, waits for them, and re-layouts  0.63 us (2%)
    pallas_call x1, Pallas kernels, local(): pl.pallas_call(kernel, out_shape=pltpu.VMEM((NCHAN, 4, LANES), F32), in_s...  34.9 us

profile of v5, /device:TPU:1, one launch (start us, length us, event | category | flops | bytes accessed | tf_op | source)
XLA Modules:
  0.0 36.2 jit_solution(12450894220494260684)
XLA Ops:
  0.7 34.9 %cross_spectra.1 = f32[32,4,128]{2,1,0:T(4,128)S(1)} custom-call(s32[1]{0:T(128)S(6)} %copy.14.offset_hbm, s32[1,24]{1,0:T(1,128)} %source_hbm.1, s32[1,24]{1,0:T(1,128)} %receiver_hbm.1, s32[1,24]{1,0:T(1,128)} %hop_hbm.1, s32[1,24]{1,0:T(1,128)} %bitcast.7, f32[96,8,128]{2,1,0:T(8,128)} %bitcast.6, bf16[128,384]{1,0:T(8,128)(2,1)} %constant.10.clone.first_hbm, ...), custom_call_target="tpu_custom_call" | custom-call | tf_op jit(solution)/shard_map/cross_spectra/pallas_call | solution.py:368
  35.5 0.6 %copy.13 = f32[64,2,128]{2,1,0:T(2,128)} copy(f32[64,2,128]{2,1,0:T(2,128)S(1)} %bitcast.5) | data formatting | bytes 131072
